TPU v7x, 256 devices: a whole 4x4x8 slice. The times are simulated.
256 devices in a mesh: wide: 16 (over y_hi, z), narrow: 16 (over y_lo, x, core).
Axes of the slice: x: 4, y: 4 (y_hi: 2, y_lo: 2; y = y_hi * 2 + y_lo), z: 8, core: 2. Of those that a mesh axis runs over, the one named last changes fastest.
Arguments:
- quantized_inputs: bfloat16 [16384, 3072], P(('wide', 'narrow')), may hold values from -6 to 6
- x_full: bfloat16 [16384, 3072], P(('wide', 'narrow')), may hold values from -6 to 6
Outputs:
- gram_out: float32 [16, 16, 64, 16384], P(None, 'narrow', None, 'wide')
- cross_gram_result: float32 [16, 16, 64, 16384], P(None, 'narrow', None, 'wide')
All inputs are finite; a program needn't handle non-finite values.
Results may differ from a plain program's by a relative error of at most 0.003.
Values may be sent and summed in bfloat16 or wider, within the bound.
A program may use at most 128 MiB of HBM per device.

v0:
```python
import jax
import jax.numpy as jnp
from jax import lax
from jax.sharding import PartitionSpec as P


def fetch_left(stacked_parts):
    return lax.all_gather(stacked_parts, "wide", axis=1, tiled=True)


def load_right_operand(quantized_inputs):
    return lax.all_gather(quantized_inputs, "narrow", axis=0, tiled=True)


def finish_left(left_pair):
    difference = (left_pair[1].astype(jnp.float32) - left_pair[0].astype(jnp.float32)).astype(
        jnp.bfloat16
    )
    return jnp.stack([left_pair[0], difference])


def per_device(quantized_inputs, x_full):
    token_count = quantized_inputs.shape[1]
    owned_rows = quantized_inputs.shape[0]
    stacked_parts = jnp.stack([quantized_inputs, x_full])
    left_operand_block = finish_left(fetch_left(stacked_parts))
    reduced_sum = jnp.einsum(
        "yia,ea->yie",
        left_operand_block,
        load_right_operand(quantized_inputs),
        preferred_element_type=jnp.float32,
    )
    tile_pairs = reduced_sum / token_count
    wide_count = lax.axis_size("wide")
    gram_out = tile_pairs[0].reshape(wide_count, 1, owned_rows, tile_pairs.shape[2])
    cross_gram_result = tile_pairs[1].reshape(wide_count, 1, owned_rows, tile_pairs.shape[2])
    return (gram_out, cross_gram_result)


def solution(mesh):
    return jax.shard_map(
        per_device,
        mesh=mesh,
        in_specs=(P(("wide", "narrow"), None), P(("wide", "narrow"), None)),
        out_specs=(P(None, "narrow", None, "wide"), P(None, "narrow", None, "wide")),
        check_vma=False,
    )
```

profile of v0, /device:TPU:6, one launch (start us, length us, event | category | flops | bytes accessed | tf_op | source)
XLA Modules:
  0.0 264.9 jit_solution(11795607325035281137)
XLA Ops:
  7.2 0.0 all-gather.3.cloned.1.call-start
  7.2 2.1 pad_maximum_fusion
  9.3 0.0 all-gather.3.cloned.1.call-update
  9.3 0.0 all-gather.5.cloned.1.call-start
  9.4 0.7 all-gather.5.cloned.1.call-update
  10.1 182.4 %all-gather.3.cloned.1.call-done = bf16[2,1024,3072]{2,1,0:T(8,128)(2,1)} async-done(((bf16[2,64,3072]{2,1,0:T(8,128)(2,1)}), bf16[2,1024,3072]{2,1,0:T(8,128)(2,1)}) %all-gather.3.cloned.1.call-update) | async-done | bytes 12582928 | tf_op jit(solution)/shard_map/all_gather | solution.py:8
  192.4 0.0 copy-start
  192.4 6.6 %slice.17 = bf16[1,1024,3072]{2,1,0:T(8,128)(2,1)} slice(bf16[2,1024,3072]{2,1,0:T(8,128)(2,1)} %all-gather.3.cloned.1.call-done), slice={[0:1], [0:1024], [0:3072]} | slice | bytes 12582912 | tf_op jit(solution)/shard_map/slice | solution.py:19
  199.0 2.1 copy-done
  201.1 4.9 %subtract_convert_fusion = bf16[1,1024,3072]{2,1,0:T(8,128)(2,1)} fusion(bf16[2,1024,3072]{2,1,0:T(8,128)(2,1)S(1)} %copy-done), kind=kLoop, calls=%fused_computation.4 | loop fusion | flops 12582912 | bytes 18874368 | tf_op jit(solution)/shard_map/convert_element_type | solution.py:16
  206.0 29.7 %all-gather.5.cloned.1.call-done = bf16[1024,3072]{1,0:T(8,128)(2,1)} async-done(((bf16[64,3072]{1,0:T(8,128)(2,1)}), bf16[1024,3072]{1,0:T(8,128)(2,1)}) %all-gather.5.cloned.1.call-update) | async-done | bytes 6291472 | tf_op jit(solution)/shard_map/all_gather | solution.py:12
  235.7 18.0 %broadcast_multiply_fusion = f32[2,1024,1024]{2,1,0:T(8,128)S(1)} fusion(bf16[1024,3072]{1,0:T(8,128)(2,1)} %all-gather.5.cloned.1.call-done, bf16[1,1024,3072]{2,1,0:T(8,128)(2,1)} %subtract_convert_fusion, bf16[1,1024,3072]{2,1,0:T(8,128)(2,1)} %slice.17), kind=kOutput, calls=%fused_computation.6 | convolution fusion | flops 12893290496 | bytes 27262976 | tf_op jit(solution)/shard_map/yia,ea->yie/dot_general | solution.py:27
  253.8 4.2 %fusion.10 = (f32[1,1024,1024]{2,1,0:T(8,128)}, f32[1,1024,1024]{2,1,0:T(8,128)}) fusion(f32[2,1024,1024]{2,1,0:T(8,128)S(1)} %broadcast_multiply_fusion), kind=kLoop, calls=%fused_computation.9 | loop fusion | bytes 16777216 | tf_op jit(solution)/shard_map/slice | solution.py:36
Async XLA Ops:
  7.2 185.2 %all-gather.3.cloned.1.call-start = ((), (), s32[]{:S(2)}) async-start(), calls=%async_computation | async-start | bytes 13369344 | tf_op jit(solution)/shard_map/all_gather | solution.py:8
  9.3 226.4 %all-gather.5.cloned.1.call-start = ((), (), s32[]{:S(2)}) async-start(), calls=%async_computation.1 | async-start | bytes 6684672 | tf_op jit(solution)/shard_map/all_gather | solution.py:12
  192.4 8.7 %copy-start = (bf16[2,1024,3072]{2,1,0:T(8,128)(2,1)S(1)}, bf16[2,1024,3072]{2,1,0:T(8,128)(2,1)}, u32[]{:S(2)}) copy-start(bf16[2,1024,3072]{2,1,0:T(8,128)(2,1)} %all-gather.3.cloned.1.call-done) | copy-start | bytes 37748740
Sparse Core Ops, SparseCore 0:
  11.1 181.2 all-gather.2
  194.3 41.4 all-gather.4
where the time goes:
time: 266 us; the launch traced here: 265 us
  waiting for transfers between devices  213 us (80%)
  matrix products  18 us (7%)
  between operations  14 us (5%)
  local copies, waits for them, and re-layouts  12.9 us (5%)
  other arithmetic  6.96 us (3%)
    all_gather x1, waiting for transfers between devices, fetch_left(): return lax.all_gather(stacked_parts, 'wide', axis=1, tiled=True)  182 us
    all_gather x1, waiting for transfers between devices, load_right_operand(): return lax.all_gather(quantized_inputs, 'narrow', axis=0, tiled=True)  29.7 us
    dot_general x1, matrix products, per_device(): jnp.einsum('yia,ea->yie', left_operand_block, load_right_operand(quantize...  18 us
    slice x1, local copies, waits for them, and re-layouts, finish_left(): return jnp.stack([left_pair[0], difference])  6.59 us
  transfers between devices with their start and end apart: 2, of which 2 were waited for; matrix products, arithmetic and copies ran while one was open for 4% of the time, Pallas kernels for 0%

commit v1 on v0

v1 whole, which is shorter than its diff:
```python
import heapq

import jax
import jax.numpy as jnp
from jax import lax
from jax.experimental import pallas as pl
from jax.experimental.pallas import tpu as pltpu
from jax.sharding import PartitionSpec as P

MESH = pl.DeviceIdType.MESH
BF16 = jnp.bfloat16
F32 = jnp.float32

NZ, NX = 8, 4
Z_OFFSET = (0, -1, 1, -2, 2, -3, 3, 4)
GROUPS = ((0, 1), (1, 2), (3, 2), (5, 2), (7, 1))
OPP, OWN = 0, 1
STEP_US = 8.46


class Messages:
    def __init__(self, send_sem, recv_sem):
        self.send_sem, self.recv_sem = send_sem, recv_sem
        self.copies = []

    def make(self, src, dst, device):
        i = len(self.copies)
        copy = pltpu.make_async_remote_copy(
            src_ref=src,
            dst_ref=dst,
            send_sem=self.send_sem.at[i],
            recv_sem=self.recv_sem.at[i],
            device_id=device,
            device_id_type=MESH,
        )
        self.copies.append(copy)
        return copy


def out_times(produced):
    queue, free, landed, n = [], 0.0, {}, 0
    for tile, (at, blocks) in produced.items():
        heapq.heappush(queue, (at, n, 0, tile, blocks))
        n += 1
    while queue:
        at, _, hop, tile, blocks = heapq.heappop(queue)
        free = max(free, at) + 0.0835 * blocks
        if hop == 0:
            landed[tile] = free + 0.12
            heapq.heappush(queue, (free + 0.12, n, 1, tile, blocks))
            n += 1
    return landed


N_SEND = 14 + 12 + 4 + 16 + 40 + 64


def kernel(q_in, x_in, out, left, xs_left, right, ship, relay, own_out, send_sem, recv_sem, local_sem):
    tokens = q_in.shape[1]
    fd = q_in.shape[0]
    scale = 1.0 / tokens
    wide, narrow = lax.axis_index("wide"), lax.axis_index("narrow")
    yh, z = wide // NZ, wide % NZ
    yl, x, core = narrow // (2 * NX), (narrow // 2) % NX, narrow % 2

    def device(yh_, z_, yl_, x_, core_):
        return (yh_ * NZ + z_, (yl_ * NX + x_) * 2 + core_)

    z_up, z_down = (device(yh, (z + d) % NZ, yl, x, core) for d in (1, NZ - 1))
    x_up, x_down = (device(yh, z, yl, (x + d) % NX, core) for d in (1, NX - 1))
    partner = device(yh, z, yl, x, 1 - core)
    y_opp = device(1 - yh, z, 1 - yl, x, core)
    y_own = device(yh, z, 1 - yl, x, core)

    barrier = pltpu.get_barrier_semaphore()
    neighbours = (z_up, z_down, x_up, x_down, partner, y_opp, y_own)
    for d in neighbours:
        pl.semaphore_signal(barrier, inc=1, device_id=d, device_id_type=MESH)
    pl.semaphore_wait(barrier, len(neighbours))

    messages = Messages(send_sem, recv_sem)
    make = messages.make
    waited = set()

    def need(copy):
        if id(copy) not in waited:
            waited.add(id(copy))
            copy.wait_recv()

    locals_ = [
        pltpu.make_async_copy(q_in, left.at[0, 0], local_sem.at[0]),
        pltpu.make_async_copy(x_in, xs_left.at[0], local_sem.at[1]),
        pltpu.make_async_copy(q_in, right.at[1, OWN, 0, core], local_sem.at[2]),
    ]

    z_msgs = {}
    for up in (True, False):
        to = z_up if up else z_down
        for k in (1, 2, 3, 4):
            src_slot = 0 if k == 1 else (2 * (k - 1) - 1 if up else 2 * (k - 1))
            dst_slot = 7 if k == 4 else (2 * k - 1 if up else 2 * k)
            if k < 4 or up:
                src = q_in if k == 1 else left.at[src_slot, 0]
                z_msgs[up, k, "q"] = make(src, left.at[dst_slot, 0], to)
            if k < 4 or not up:
                src = x_in if k == 1 else xs_left.at[src_slot]
                z_msgs[up, k, "x"] = make(src, xs_left.at[dst_slot], to)

    def left_messages(slot):
        if slot == 0:
            return []
        if slot == 7:
            return [z_msgs[True, 4, "q"], z_msgs[False, 4, "x"]]
        up, k = slot % 2 == 1, (slot + 1) // 2
        return [z_msgs[up, k, "q"], z_msgs[up, k, "x"]]

    half = fd // 2
    lo, hi = pl.ds(0, half), pl.ds(half, half)
    y_to_opp = make(q_in, right.at[1, OPP, 1, core], y_opp)
    y_to_own = make(q_in, right.at[1, OWN, 1, core], y_own)
    y_two_a = make(right.at[1, OPP, 1, core, lo], right.at[1, OPP, 0, core, lo], y_own)
    y_two_b = make(right.at[1, OWN, 1, core, hi], right.at[1, OPP, 0, core, hi], y_opp)

    x_msgs = {}
    for hy in (OPP, OWN):
        for ly in (0, 1):
            src = q_in if (hy, ly) == (OWN, 0) else right.at[1, hy, ly, core]
            x_msgs["up", hy, ly] = make(src, right.at[0, hy, ly, core], x_up)
            x_msgs["down", hy, ly] = make(src, right.at[2, hy, ly, core], x_down)
    for hy, ly in ((OPP, 1), (OWN, 0)):
        x_msgs["far", hy, ly] = make(right.at[0, hy, ly, core], right.at[3, hy, ly, core], x_up)
    for hy, ly in ((OPP, 0), (OWN, 1)):
        x_msgs["far", hy, ly] = make(right.at[2, hy, ly, core], right.at[3, hy, ly, core], x_down)

    p_msgs = {}
    for xs in range(4):
        for hy in (OPP, OWN):
            for ly in (0, 1):
                src = q_in if (xs, hy, ly) == (1, OWN, 0) else right.at[xs, hy, ly, core]
                p_msgs[xs, hy, ly] = make(src, right.at[xs, hy, ly, core], partner)

    x_way = {0: "up", 2: "down", 3: "far"}

    def right_messages(xs, hy):
        got = [p_msgs[xs, hy, ly] for ly in (0, 1)]
        if xs != 1:
            return [x_msgs[x_way[xs], hy, ly] for ly in (0, 1)] + got
        if hy == OPP:
            return [y_to_opp, y_two_a, y_two_b] + got
        return [y_to_own] + got

    first, second = {}, {}
    for g, (l0, nl) in enumerate(GROUPS):
        for xs in range(4):
            for path in (0, 1):
                rows = pl.ds(l0, nl)
                first[g, xs, path] = make(
                    ship.at[path, xs, rows], relay.at[path, xs, rows], (y_opp, y_own)[path]
                )
                src_yh = 1 - yh if path == 0 else yh
                col_yl = 1 - yl if path == 0 else yl
                col = pl.multiple_of(col_yl * (2 * NX * fd) + ((x + xs + NX - 1) % NX) * (2 * fd), 2 * fd)
                second[g, xs, path] = [
                    make(
                        relay.at[path, xs, l],
                        out.at[:, src_yh * NZ + (z + Z_OFFSET[l] + NZ) % NZ, :, pl.ds(col, 2 * fd)],
                        (y_own, y_opp)[path],
                    )
                    for l in range(l0, l0 + nl)
                ]
    assert len(messages.copies) == N_SEND, len(messages.copies)

    have_diff = set()

    def diff(slot):
        if slot in have_diff:
            return
        have_diff.add(slot)
        if slot == 0:
            locals_[0].wait()
            locals_[1].wait()
        for m in left_messages(slot):
            need(m)
        left[slot, 1] = (xs_left[slot].astype(F32) - left[slot, 0].astype(F32)).astype(BF16)

    have_own = []

    def ready(g, xs_list, hy):
        l0, nl = GROUPS[g]
        for slot in range(l0, l0 + nl):
            diff(slot)
        for xs in xs_list:
            if (xs, hy) == (1, OWN) and not have_own:
                have_own.append(1)
                locals_[2].wait()
            for m in right_messages(xs, hy):
                need(m)

    def product(l0, nl, xs, hy):
        a = left[pl.ds(l0, nl)].reshape(nl * 2 * fd, tokens)
        b = right[xs, hy].reshape(4 * fd, tokens)
        p = lax.dot_general(a, b, (((1,), (1,)), ((), ())), preferred_element_type=F32) * scale
        return p.astype(BF16).reshape(nl, 2, fd, 4 * fd)

    def opp_tile(g, xs):
        l0, nl = GROUPS[g]
        p = product(l0, nl, xs, OPP)
        for path in (0, 1):
            ship[path, xs, l0 : l0 + nl] = p[..., path * 2 * fd : (path + 1) * 2 * fd]

    def own_tiles(g, start, step, count):
        l0, nl = GROUPS[g]

        def one(i, _):
            xs = start + i * step
            p = product(l0, nl, xs, OWN)
            for ly in (0, 1):
                col_yl = yl if ly == 0 else 1 - yl
                col = pl.multiple_of(col_yl * (2 * NX * fd) + ((x + xs + NX - 1) % NX) * (2 * fd), 2 * fd)
                own_out[l0 : l0 + nl, :, :, pl.ds(col, 2 * fd)] = p[..., ly * 2 * fd : (ly + 1) * 2 * fd]
            return 0

        if count == 1:
            one(0, 0)
        else:
            lax.fori_loop(0, count, one, 0)

    events = []

    def at(time, fn):
        events.append((time, len(events), fn))

    def forward_z(what, k):
        def go():
            for up in (True, False):
                if (up, k, what) in z_msgs:
                    need(z_msgs[up, k, what])
                if (up, k + 1, what) in z_msgs:
                    z_msgs[up, k + 1, what].start()

        return go

    for k in (1, 2, 3):
        at(2 * k - 1 + 0.02, forward_z("q", k))
        at(2 * k + 0.02, forward_z("x", k))

    def start_all():
        for key in ((True, 1, "q"), (False, 1, "q")):
            z_msgs[key].start()
        y_to_opp.start()
        y_to_own.start()
        x_msgs["up", OWN, 0].start()
        x_msgs["down", OWN, 0].start()
        p_msgs[1, OWN, 0].start()
        for key in ((True, 1, "x"), (False, 1, "x")):
            z_msgs[key].start()
        for c in locals_:
            c.start()

    at(0.0, start_all)

    def y_arrived():
        need(y_to_opp)
        y_two_a.start()
        x_msgs["up", OPP, 1].start()
        x_msgs["down", OPP, 1].start()
        p_msgs[1, OPP, 1].start()
        need(y_to_own)
        y_two_b.start()
        p_msgs[1, OWN, 1].start()

    at(1.0, y_arrived)

    def y_two_arrived():
        need(y_two_a)
        need(y_two_b)
        x_msgs["up", OPP, 0].start()
        x_msgs["down", OPP, 0].start()
        p_msgs[1, OPP, 0].start()

    at(1.5, y_two_arrived)

    def x_arrived(hy, ly, then=()):
        def go():
            need(x_msgs["up", hy, ly])
            if (hy, ly) == (OPP, 1):
                x_msgs["far", hy, ly].start()
            p_msgs[0, hy, ly].start()
            need(x_msgs["down", hy, ly])
            if (hy, ly) in ((OPP, 0), (OWN, 1)):
                x_msgs["far", hy, ly].start()
            p_msgs[2, hy, ly].start()
            for m in then:
                x_msgs[m].start()

        return go

    at(1.03, x_arrived(OWN, 0))
    at(2.03, x_arrived(OPP, 1, (("up", OWN, 1),)))
    at(3.03, x_arrived(OPP, 0, (("down", OWN, 1), ("far", OWN, 0))))
    at(5.03, x_arrived(OWN, 1))

    def far_arrived(pairs):
        def go():
            for hy, ly in pairs:
                need(x_msgs["far", hy, ly])
                p_msgs[3, hy, ly].start()

        return go

    at(4.03, far_arrived(((OPP, 1), (OPP, 0))))
    at(6.03, far_arrived(((OWN, 0), (OWN, 1))))

    produced, pending, sent = {}, [], set()

    def flush():
        while pending:
            tile = pending.pop()
            sent.add(tile)
            for path in (0, 1):
                first[tile + (path,)].start()

    def opp_at(time, g, xs):
        def go():
            ready(g, (xs,), OPP)
            before = list(pending)
            opp_tile(g, xs)
            if before:
                flush()
            pending.append((g, xs))

        at(time, go)
        produced[g, xs] = (time + 0.12, GROUPS[g][1])

    def own_at(time, g, start, step, count):
        def go():
            ready(g, [start + i * step for i in range(count)], OWN)
            own_tiles(g, start, step, count)
            flush()

        at(time, go)

    opp_at(1.70, 0, 1)
    own_at(1.75, 0, 1, 1, 1)
    opp_at(2.10, 1, 1)
    own_at(2.20, 1, 1, 1, 1)
    for i, xs in enumerate((0, 2)):
        opp_at(3.10 + 0.15 * i, 0, xs)
        opp_at(3.16 + 0.15 * i, 1, xs)
    for i, (g, xs) in enumerate(((2, 1), (2, 0), (2, 2), (0, 3), (1, 3), (2, 3))):
        opp_at(4.10 + 0.1 * i, g, xs)
    own_at(4.72, 2, 1, 1, 1)
    own_at(5.12, 0, 0, 2, 2)
    own_at(5.30, 1, 0, 2, 2)
    own_at(5.50, 2, 0, 2, 2)
    for xs in range(4):
        opp_at(6.10 + 0.1 * xs, 3, xs)
    own_at(6.51, 0, 3, 1, 1)
    own_at(6.56, 1, 3, 1, 1)
    own_at(6.66, 2, 3, 1, 1)
    own_at(6.76, 3, 0, 1, 4)
    for xs in range(4):
        opp_at(7.10 + 0.05 * xs, 4, xs)
    own_at(7.31, 4, 0, 1, 4)

    def relay_at(time, tile):
        def go():
            if tile not in sent:
                flush()
            for path in (0, 1):
                need(first[tile + (path,)])
                for m in second[tile + (path,)]:
                    m.start()

        at(time, go)

    for tile, time in out_times(produced).items():
        relay_at(time, tile)

    own_copies = []

    def write_own(slots):
        def go():
            for l in slots:
                c = pltpu.make_async_copy(
                    own_out.at[l], out.at[:, yh * NZ + (z + Z_OFFSET[l] + NZ) % NZ], local_sem.at[3 + l]
                )
                c.start()
                own_copies.append(c)

        return go

    at(7.05, write_own(range(7)))
    at(7.45, write_own((7,)))

    for _, _, fn in sorted(events, key=lambda e: e[:2]):
        fn()

    for group in second.values():
        for m in group:
            need(m)
    for c in own_copies:
        c.wait()
    for m in messages.copies:
        m.wait_send()
        if id(m) not in waited:
            raise ValueError("unreceived message")


def per_device(quantized_inputs, x_full):
    fd, tokens = quantized_inputs.shape
    columns = 16 * fd
    stats = pl.pallas_call(
        kernel,
        out_shape=jax.ShapeDtypeStruct((2, 16, fd, columns), BF16),
        in_specs=[pl.BlockSpec(memory_space=pl.ANY)] * 2,
        out_specs=pl.BlockSpec(memory_space=pl.ANY),
        scratch_shapes=[
            pltpu.VMEM((8, 2, fd, tokens), BF16),
            pltpu.VMEM((8, fd, tokens), BF16),
            pltpu.VMEM((4, 2, 2, 2, fd, tokens), BF16),
            pltpu.VMEM((2, 4, 8, 2, fd, 2 * fd), BF16),
            pltpu.VMEM((2, 4, 8, 2, fd, 2 * fd), BF16),
            pltpu.VMEM((8, 2, fd, columns), BF16),
            pltpu.SemaphoreType.DMA((N_SEND,)),
            pltpu.SemaphoreType.DMA((N_SEND,)),
            pltpu.SemaphoreType.DMA((11,)),
        ],
        compiler_params=pltpu.CompilerParams(collective_id=0, has_side_effects=True),
    )(quantized_inputs, x_full)
    shape = (16, 1, fd, columns)
    return stats[0].astype(F32).reshape(shape), stats[1].astype(F32).reshape(shape)


def solution(mesh):
    return jax.shard_map(
        per_device,
        mesh=mesh,
        in_specs=(P(("wide", "narrow"), None), P(("wide", "narrow"), None)),
        out_specs=(P(None, "narrow", None, "wide"), P(None, "narrow", None, "wide")),
        check_vma=False,
    )
```

time: 266 us -> 104 us (0.39)
  waiting for transfers between devices: 213 us -> 0 us
  Pallas kernels: 0 us -> 96.9 us
  matrix products: 18 us -> 0 us
  between operations: 14 us -> 0.64 us
  local copies, waits for them, and re-layouts: 12.9 us -> 0 us
    all_gather x2 -> x0, waiting for transfers between devices: 212 us -> none  [the longest x1 182 us: fetch_left(): return lax.all_gather(stacked_parts, 'wide', axis=1, tiled=True)]
    pallas_call x0 -> x1, Pallas kernels: none -> 96.9 us  [per_device(): pl.pallas_call(kernel, out_shape=jax.ShapeDtypeStruct((2, 16, fd, columns...]
    dot_general x1 -> x0, matrix products: 18 us -> none  [per_device(): jnp.einsum('yia,ea->yie', left_operand_block, load_right_operand(quantize...]
    slice x2 -> x0, local copies, waits for them, and re-layouts: 10.8 us -> none  [the longest x1 6.59 us: finish_left(): return jnp.stack([left_pair[0], difference])]
    unnamed x0 -> x1, other arithmetic: none -> 6.69 us
    convert_element_type x1 -> x0, other arithmetic: 4.9 us -> none  [finish_left(): (left_pair[1].astype(jnp.float32) - left_pair[0].astype(jnp.float32)).ast...]
  transfers between devices with their start and end apart: 2 -> 0, of which waited for: 2 -> 0; matrix products, arithmetic and copies ran while one was open for 4% -> 0% of each run, Pallas kernels for 0% -> 0%
where the time goes in v1:
time: 104 us
  Pallas kernels  96.9 us (93%)
  other arithmetic  6.69 us (6%)
    pallas_call x1, Pallas kernels, per_device(): pl.pallas_call(kernel, out_shape=jax.ShapeDtypeStruct((2, 16, fd, columns...  96.9 us
    unnamed x1, other arithmetic  6.69 us

profile of v1, /device:TPU:6, one launch (start us, length us, event | category | flops | bytes accessed | tf_op | source)
XLA Modules:
  0.0 104.2 jit_solution(1522336389956578242)
XLA Ops:
  0.6 96.9 %shard_map.41 = bf16[2,16,64,1024]{3,2,1,0:T(8,128)(2,1)} custom-call(bf16[64,3072]{1,0:T(8,128)(2,1)} %q_in.1, bf16[64,3072]{1,0:T(8,128)(2,1)} %x_in.1), custom_call_target="tpu_custom_call" | custom-call | tf_op jit(solution)/shard_map/pallas_call | solution.py:413
  97.5 6.7 %bitcast_convert_fusion = (f32[16,1,64,1024]{3,2,1,0:T(8,128)}, f32[16,1,64,1024]{3,2,1,0:T(8,128)}) fusion(bf16[2,16,64,1024]{3,2,1,0:T(8,128)(2,1)} %shard_map.41), kind=kLoop, calls=%fused_computation | loop fusion | flops 2097152 | bytes 12582912

commit v2 on v0

v2 whole, which is shorter than its diff:
```python
import heapq

import jax
import jax.numpy as jnp
from jax import lax
from jax.experimental import pallas as pl
from jax.experimental.pallas import tpu as pltpu
from jax.sharding import PartitionSpec as P

MESH = pl.DeviceIdType.MESH
BF16 = jnp.bfloat16
F32 = jnp.float32

NZ, NX = 8, 4
Z_OFFSET = (0, -1, 1, -2, 2, -3, 3, 4)
Q_AT = (0, 2, 3, 6, 7, 10, 11, 14)
D_AT = (1, 4, 5, 8, 9, 12, 13, 15)
OPP, OWN = 0, 1
BLOCK = 0.0417


def out_times(produced):
    queue, free, landed, n = [], [0.0, 0.0], {}, 0
    for tile, at in produced.items():
        heapq.heappush(queue, (at, n, 0, tile))
        n += 1
    while queue:
        at, _, hop, tile = heapq.heappop(queue)
        link = tile[0] if hop == 0 else 1 - tile[0]
        free[link] = max(free[link], at) + BLOCK * (tile[3] if tile[4] is None else tile[3] / 2)
        if hop == 0:
            landed[tile] = free[link] + 0.15
            heapq.heappush(queue, (landed[tile], n, 1, tile))
            n += 1
    return landed


N_RING = 16 + 12 + 4 + 16
N_OUT = 58
Z_SEND, X_SEND, Y_SEND, P_SEND, SHIP_SEND, RELAY_SEND = range(6)


def gather_kernel(
    q_in, x_in, out, left, xs_left, right, ship, relay, send_sem, ring_sem, ship_sem, out_sem, local_sem
):
    fd, tokens = q_in.shape
    half = fd // 2
    scale = 1.0 / tokens
    wide, narrow = lax.axis_index("wide"), lax.axis_index("narrow")
    yh, z = wide // NZ, wide % NZ
    yl, x, core = narrow // (2 * NX), (narrow // 2) % NX, narrow % 2

    def device(yh_, z_, yl_, x_, core_):
        return (yh_ * NZ + z_, (yl_ * NX + x_) * 2 + core_)

    z_up, z_down = (device(yh, (z + d) % NZ, yl, x, core) for d in (1, NZ - 1))
    x_up, x_down = (device(yh, z, yl, (x + d) % NX, core) for d in (1, NX - 1))
    partner = device(yh, z, yl, x, 1 - core)
    y_opp = device(1 - yh, z, 1 - yl, x, core)
    y_own = device(yh, z, 1 - yl, x, core)

    barrier = pltpu.get_barrier_semaphore()
    neighbours = (z_up, z_down, x_up, x_down, partner, y_opp, y_own)
    for d in neighbours:
        pl.semaphore_signal(barrier, inc=1, device_id=d, device_id_type=MESH)
    pl.semaphore_wait(barrier, len(neighbours))

    ring_count = [0]
    waited = set()

    def copy(src, dst, sender, receive, to):
        return pltpu.make_async_remote_copy(
            src_ref=src,
            dst_ref=dst,
            send_sem=send_sem.at[sender],
            recv_sem=receive,
            device_id=to,
            device_id_type=MESH,
        )

    def make(src, dst, sender, to):
        ring_count[0] += 1
        return copy(src, dst, sender, ring_sem.at[ring_count[0] - 1], to)

    def need(m):
        if id(m) not in waited:
            waited.add(id(m))
            m.wait_recv()

    locals_ = [
        pltpu.make_async_copy(q_in, left.at[0], local_sem.at[0]),
        pltpu.make_async_copy(x_in, xs_left.at[0], local_sem.at[1]),
        pltpu.make_async_copy(q_in, right.at[1, OWN, 0, core], local_sem.at[2]),
    ]

    lo, hi = pl.ds(0, half), pl.ds(half, half)

    z_msgs = {}
    for up in (True, False):
        to = z_up if up else z_down
        for k in (1, 2, 3):
            src, dst = (2 * (k - 1) - 1 if up else 2 * (k - 1)), (2 * k - 1 if up else 2 * k)
            q_src = q_in if k == 1 else left.at[Q_AT[src]]
            x_src = x_in if k == 1 else xs_left.at[src]
            z_msgs[up, k, "q"] = make(q_src, left.at[Q_AT[dst]], Z_SEND, to)
            z_msgs[up, k, "x"] = make(x_src, xs_left.at[dst], Z_SEND, to)
        for h, rows in enumerate((lo, hi)):
            if up:
                z_msgs[up, 4, "q", h] = make(left.at[Q_AT[5], rows], left.at[Q_AT[7], rows], Z_SEND, to)
            else:
                z_msgs[up, 4, "x", h] = make(xs_left.at[6, rows], xs_left.at[7, rows], Z_SEND, to)

    y_to_opp = make(q_in, right.at[1, OPP, 1, core], Y_SEND, y_opp)
    y_to_own = make(q_in, right.at[1, OWN, 1, core], Y_SEND, y_own)
    y_two_a = make(right.at[1, OPP, 1, core, lo], right.at[1, OPP, 0, core, lo], Y_SEND, y_own)
    y_two_b = make(right.at[1, OWN, 1, core, hi], right.at[1, OPP, 0, core, hi], Y_SEND, y_opp)

    x_msgs = {}
    for hy in (OPP, OWN):
        for ly in (0, 1):
            src = q_in if (hy, ly) == (OWN, 0) else right.at[1, hy, ly, core]
            x_msgs["up", hy, ly] = make(src, right.at[0, hy, ly, core], X_SEND, x_up)
            x_msgs["down", hy, ly] = make(src, right.at[2, hy, ly, core], X_SEND, x_down)
    for hy, ly in ((OPP, 1), (OWN, 0)):
        x_msgs["far", hy, ly] = make(right.at[0, hy, ly, core], right.at[3, hy, ly, core], X_SEND, x_up)
    for hy, ly in ((OPP, 0), (OWN, 1)):
        x_msgs["far", hy, ly] = make(right.at[2, hy, ly, core], right.at[3, hy, ly, core], X_SEND, x_down)

    p_msgs = {}
    for xs in range(4):
        for hy in (OPP, OWN):
            for ly in (0, 1):
                src = q_in if (xs, hy, ly) == (1, OWN, 0) else right.at[xs, hy, ly, core]
                p_msgs[xs, hy, ly] = make(src, right.at[xs, hy, ly, core], P_SEND, partner)
    assert ring_count[0] == N_RING, ring_count[0]

    x_way = {0: "up", 2: "down", 3: "far"}

    def right_messages(xs, hy, ly):
        got = [p_msgs[xs, hy, ly]]
        if xs != 1:
            return [x_msgs[x_way[xs], hy, ly]] + got
        if ly == 0:
            return ([y_two_a, y_two_b] if hy == OPP else []) + got
        return [y_to_opp if hy == OPP else y_to_own] + got

    def block(ref, tile):
        path, xs, r0, n, h = tile
        if h is None:
            return ref.at[path, xs, pl.ds(r0, n)]
        return ref.at[path, xs, pl.ds(r0, n), pl.ds(h * half, half)]

    first, second = {}, {}

    def plan(tile):
        to = (y_opp, y_own)
        first[tile] = copy(
            block(ship, tile), block(relay, tile), SHIP_SEND, ship_sem.at[len(first)], to[tile[0]]
        )
        second[tile] = copy(
            block(relay, tile), block(out.at[1], tile), RELAY_SEND, out_sem.at[0], to[1 - tile[0]]
        )

    have = set()

    def once(key, fn):
        if key not in have:
            have.add(key)
            fn()

    def subtract(slot, rows):
        left[D_AT[slot], rows] = (xs_left[slot, rows].astype(F32) - left[Q_AT[slot], rows].astype(F32)).astype(
            BF16
        )

    def left_ready(r0, n, h):
        for r in range(r0, r0 + n):
            if r >= 14:
                for i in (0, 1) if h is None else (h,):
                    need(z_msgs[True, 4, "q", i])
                    need(z_msgs[False, 4, "x", i])
                    once(("d", 7, i), lambda i=i: subtract(7, pl.ds(i * half, half)))
            elif r == 0:
                once("q", locals_[0].wait)
            elif r in Q_AT:
                slot = Q_AT.index(r)
                need(z_msgs[slot % 2 == 1, (slot + 1) // 2, "q"])
            else:
                slot = D_AT.index(r)
                if slot == 0:
                    once("q", locals_[0].wait)
                    once("x", locals_[1].wait)
                else:
                    need(z_msgs[slot % 2 == 1, (slot + 1) // 2, "q"])
                    need(z_msgs[slot % 2 == 1, (slot + 1) // 2, "x"])
                once(("d", slot), lambda slot=slot: subtract(slot, pl.ds(0, fd)))

    def right_ready(xs, hy, lys):
        for ly in lys:
            if (xs, hy, ly) == (1, OWN, 0):
                once("r", locals_[2].wait)
            for m in right_messages(xs, hy, ly):
                need(m)

    def product(xs, hy, lys, r0, n, h):
        if h is None:
            a = left[r0 : r0 + n].reshape(n * fd, tokens)
        else:
            a = left[r0 : r0 + n, h * half : (h + 1) * half].reshape(n * half, tokens)
        b = right[xs, hy, lys[0] : lys[-1] + 1].reshape(len(lys) * 2 * fd, tokens)
        p = lax.dot_general(a, b, (((1,), (1,)), ((), ())), preferred_element_type=F32) * scale
        return p.astype(BF16).reshape(n, fd if h is None else half, len(lys) * 2 * fd)

    def own_tiles(r0, n, start, step, count):
        def one(i, _):
            xs = start + i * step
            p = product(xs, OWN, (0, 1), r0, n, None)
            for ly in (0, 1):
                out[0, ly, xs, r0 : r0 + n] = p[..., ly * 2 * fd : (ly + 1) * 2 * fd]
            return 0

        if count == 1:
            one(0, 0)
        else:
            lax.fori_loop(0, count, one, 0)

    events = []

    def at(time, fn):
        events.append((time, len(events), fn))

    def forward_z(what, k):
        def go():
            for up in (True, False):
                need(z_msgs[up, k, what])
                if k < 3:
                    z_msgs[up, k + 1, what].start()
                elif up == (what == "q"):
                    z_msgs[up, 4, what, 0].start()
                    z_msgs[up, 4, what, 1].start()

        return go

    for k in (1, 2, 3):
        at(2 * k - 1 + 0.05, forward_z("q", k))
        at(2 * k + 0.05, forward_z("x", k))

    def start_all():
        for key in ((True, 1, "q"), (False, 1, "q")):
            z_msgs[key].start()
        y_to_opp.start()
        y_to_own.start()
        x_msgs["up", OWN, 0].start()
        x_msgs["down", OWN, 0].start()
        p_msgs[1, OWN, 0].start()
        for key in ((True, 1, "x"), (False, 1, "x")):
            z_msgs[key].start()
        for c in locals_:
            c.start()

    at(0.0, start_all)

    def y_arrived():
        need(y_to_opp)
        y_two_a.start()
        x_msgs["up", OPP, 1].start()
        x_msgs["down", OPP, 1].start()
        p_msgs[1, OPP, 1].start()
        need(y_to_own)
        y_two_b.start()
        p_msgs[1, OWN, 1].start()

    at(1.04, y_arrived)

    def y_two_arrived():
        need(y_two_a)
        need(y_two_b)
        x_msgs["up", OPP, 0].start()
        x_msgs["down", OPP, 0].start()
        p_msgs[1, OPP, 0].start()

    at(1.6, y_two_arrived)

    def x_arrived(hy, ly, then=()):
        def go():
            need(x_msgs["up", hy, ly])
            if (hy, ly) == (OPP, 1):
                x_msgs["far", hy, ly].start()
            p_msgs[0, hy, ly].start()
            need(x_msgs["down", hy, ly])
            if (hy, ly) in ((OPP, 0), (OWN, 1)):
                x_msgs["far", hy, ly].start()
            p_msgs[2, hy, ly].start()
            for m in then:
                x_msgs[m].start()

        return go

    at(1.06, x_arrived(OWN, 0))
    at(2.15, x_arrived(OPP, 1, (("up", OWN, 1),)))
    at(3.2, x_arrived(OPP, 0, (("down", OWN, 1), ("far", OWN, 0))))
    at(5.3, x_arrived(OWN, 1))

    def far_arrived(pairs):
        def go():
            for hy, ly in pairs:
                need(x_msgs["far", hy, ly])
                p_msgs[3, hy, ly].start()

        return go

    at(4.25, far_arrived(((OPP, 1), (OPP, 0))))
    at(6.35, far_arrived(((OWN, 0), (OWN, 1))))

    produced, pending, sent = {}, [], set()

    def flush():
        while pending:
            tile = pending.pop(0)
            sent.add(tile)
            first[tile].start()

    def opp_at(time, r0, n, xs, lys=(0, 1), h=None):
        tiles = [(ly, xs, r0, n, h) for ly in lys]

        def go():
            left_ready(r0, n, h)
            right_ready(xs, OPP, lys)
            before = list(pending)
            p = product(xs, OPP, lys, r0, n, h)
            for i, tile in enumerate(tiles):
                value = p[..., i * 2 * fd : (i + 1) * 2 * fd]
                if h is None:
                    ship[tile[0], xs, r0 : r0 + n] = value
                else:
                    ship[tile[0], xs, r0 : r0 + n, h * half : (h + 1) * half] = value
            if before:
                flush()
            pending.extend(tiles)

        at(time, go)
        for tile in tiles:
            plan(tile)
            produced[tile] = time + 0.1

    def own_at(time, r0, n, start, step, count):
        def go():
            left_ready(r0, n, None)
            for i in range(count):
                right_ready(start + i * step, OWN, (0, 1))
            own_tiles(r0, n, start, step, count)
            flush()

        at(time, go)

    opp_at(1.75, 0, 2, 1)
    own_at(1.76, 0, 2, 1, 1, 1)
    opp_at(2.10, 2, 4, 1)
    for i, xs in enumerate((0, 2)):
        opp_at(2.32 + 0.08 * i, 0, 6, xs, (1,))
    own_at(2.50, 2, 4, 1, 1, 1)
    opp_at(3.10, 6, 2, 1)
    for i, xs in enumerate((0, 2)):
        opp_at(3.36 + 0.13 * i, 0, 6, xs, (0,))
        opp_at(3.44 + 0.13 * i, 6, 2, xs)
    for i, xs in enumerate((1, 0, 2)):
        opp_at(4.10 + 0.05 * i, 8, 2, xs)
    opp_at(4.42, 0, 4, 3)
    opp_at(4.49, 4, 4, 3)
    opp_at(4.56, 8, 2, 3)
    own_at(4.70, 6, 4, 1, 1, 1)
    for i, xs in enumerate((1, 0, 2, 3)):
        opp_at(5.10 + 0.05 * i, 10, 2, xs)
    own_at(5.50, 0, 4, 0, 2, 2)
    own_at(5.66, 4, 4, 0, 2, 2)
    own_at(5.80, 8, 2, 0, 2, 2)
    for i, xs in enumerate((1, 0, 2, 3)):
        opp_at(6.10 + 0.05 * i, 12, 2, xs)
    own_at(6.31, 10, 4, 0, 1, 3)
    for h in (0, 1):
        for i, xs in enumerate((1, 0, 2, 3)):
            opp_at(6.60 + 0.5 * h + 0.05 * i, 14, 2, xs, (0, 1), h)
    own_at(7.31, 14, 2, 0, 1, 3)
    own_at(7.42, 0, 4, 3, 1, 1)
    own_at(7.49, 4, 4, 3, 1, 1)
    own_at(7.56, 8, 4, 3, 1, 1)
    own_at(7.63, 12, 4, 3, 1, 1)
    assert len(first) == N_OUT, len(first)

    def relay_at(time, tile):
        def go():
            if tile not in sent:
                flush()
            need(first[tile])
            second[tile].start()

        at(time, go)

    for tile, time in out_times(produced).items():
        relay_at(time, tile)

    for _, _, fn in sorted(events, key=lambda e: e[:2]):
        fn()

    def finish(ref, sender):
        copy(ref, ref, sender, out_sem.at[0], z_up).wait_send()

    copy(out.at[1], out.at[1], RELAY_SEND, out_sem.at[0], z_up).wait_recv()
    finish(left.at[pl.ds(0, 14)], Z_SEND)
    finish(left.at[pl.ds(0, 12)], X_SEND)
    finish(left.at[pl.ds(0, 3)], Y_SEND)
    finish(left.at[pl.ds(0, 16)], P_SEND)
    finish(ship, SHIP_SEND)
    finish(relay, RELAY_SEND)


def widen_kernel(stats, gram, cross, stage, sem):
    fd = stats.shape[4]
    wide, narrow = lax.axis_index("wide"), lax.axis_index("narrow")
    yh, z = wide // NZ, wide % NZ
    yl, x = narrow // (2 * NX), (narrow // 2) % NX
    copies = []
    for src in (0, 1):
        src_yh = yh if src == 0 else 1 - yh
        for slot in range(NZ):
            row = src_yh * NZ + (z + Z_OFFSET[slot] + NZ) % NZ
            for what, (at, dst) in enumerate(((Q_AT, gram), (D_AT, cross))):
                for ly in (0, 1):
                    col_yl = yl if ly == 0 else 1 - yl
                    for xs in range(4):
                        col = col_yl * (2 * NX * fd) + ((x + xs + NX - 1) % NX) * (2 * fd)
                        stage[what, src * NZ + slot, :, pl.ds(pl.multiple_of(col, 2 * fd), 2 * fd)] = stats[
                            src, ly, xs, at[slot]
                        ].astype(F32)
                i = what * 2 * NZ + src * NZ + slot
                c = pltpu.make_async_copy(stage.at[what, src * NZ + slot], dst.at[row, 0], sem.at[i])
                c.start()
                copies.append(c)
    for c in copies:
        c.wait()


def per_device(quantized_inputs, x_full):
    fd, tokens = quantized_inputs.shape
    columns = 16 * fd
    half_out = (2, 4, 16, fd, 2 * fd)
    stats = pl.pallas_call(
        gather_kernel,
        out_shape=pltpu.VMEM((2,) + half_out, BF16),
        in_specs=[pl.BlockSpec(memory_space=pltpu.HBM)] * 2,
        out_specs=pl.BlockSpec(memory_space=pltpu.VMEM),
        scratch_shapes=[
            pltpu.VMEM((16, fd, tokens), BF16),
            pltpu.VMEM((8, fd, tokens), BF16),
            pltpu.VMEM((4, 2, 2, 2, fd, tokens), BF16),
            pltpu.VMEM(half_out, BF16),
            pltpu.VMEM(half_out, BF16),
            pltpu.SemaphoreType.DMA((6,)),
            pltpu.SemaphoreType.DMA((N_RING,)),
            pltpu.SemaphoreType.DMA((N_OUT,)),
            pltpu.SemaphoreType.DMA((1,)),
            pltpu.SemaphoreType.DMA((3,)),
        ],
        compiler_params=pltpu.CompilerParams(
            collective_id=0, has_side_effects=True, vmem_limit_bytes=(59 * 1024 + 640) * 1024
        ),
    )(quantized_inputs, x_full)
    shape = (16, 1, fd, columns)
    return tuple(
        pl.pallas_call(
            widen_kernel,
            out_shape=[jax.ShapeDtypeStruct(shape, F32)] * 2,
            in_specs=[pl.BlockSpec(memory_space=pltpu.VMEM)],
            out_specs=[pl.BlockSpec(memory_space=pl.ANY)] * 2,
            scratch_shapes=[
                pltpu.VMEM((2, 16, fd, columns), F32),
                pltpu.SemaphoreType.DMA((32,)),
            ],
            compiler_params=pltpu.CompilerParams(vmem_limit_bytes=24 * 2**20),
        )(stats)
    )


def solution(mesh):
    return jax.shard_map(
        per_device,
        mesh=mesh,
        in_specs=(P(("wide", "narrow"), None), P(("wide", "narrow"), None)),
        out_specs=(P(None, "narrow", None, "wide"), P(None, "narrow", None, "wide")),
        check_vma=False,
    )
```

time: 266 us -> 115 us (0.43)
  waiting for transfers between devices: 213 us -> 0 us
  Pallas kernels: 0 us -> 113 us
  matrix products: 18 us -> 0 us
  between operations: 14 us -> 0.8 us
  local copies, waits for them, and re-layouts: 12.9 us -> 0 us
  other arithmetic: 6.96 us -> 0 us
    all_gather x2 -> x0, waiting for transfers between devices: 212 us -> none  [the longest x1 182 us: fetch_left(): return lax.all_gather(stacked_parts, 'wide', axis=1, tiled=True)]
    pallas_call x0 -> x2, Pallas kernels: none -> 113 us  [the longest x1 110 us: per_device(): pl.pallas_call(gather_kernel, out_shape=pltpu.VMEM((2,) + half_out, BF16)...]
    dot_general x1 -> x0, matrix products: 18 us -> none  [per_device(): jnp.einsum('yia,ea->yie', left_operand_block, load_right_operand(quantize...]
    slice x2 -> x0, local copies, waits for them, and re-layouts: 10.8 us -> none  [the longest x1 6.59 us: finish_left(): return jnp.stack([left_pair[0], difference])]
    convert_element_type x1 -> x0, other arithmetic: 4.9 us -> none  [finish_left(): (left_pair[1].astype(jnp.float32) - left_pair[0].astype(jnp.float32)).ast...]
  transfers between devices with their start and end apart: 2 -> 0, of which waited for: 2 -> 0; matrix products, arithmetic and copies ran while one was open for 4% -> 0% of each run, Pallas kernels for 0% -> 0%
where the time goes in v2:
time: 115 us; the launch traced here: 114 us
  Pallas kernels  113 us (98%)
    pallas_call x1, Pallas kernels, per_device(): pl.pallas_call(gather_kernel, out_shape=pltpu.VMEM((2,) + half_out, BF16)...  110 us
    pallas_call x1, Pallas kernels, per_device(): pl.pallas_call(widen_kernel, out_shape=[jax.ShapeDtypeStruct(shape, F32)]...  3.59 us

profile of v2, /device:TPU:6, one launch (start us, length us, event | category | flops | bytes accessed | tf_op | source)
XLA Modules:
  0.0 114.2 jit_solution(9120960693389953882)
XLA Ops:
  0.6 109.8 %shard_map.41.stats = bf16[2,2,4,16,64,128]{5,4,3,2,1,0:T(8,128)(2,1)S(1)} custom-call(bf16[64,3072]{1,0:T(8,128)(2,1)} %q_in.1, bf16[64,3072]{1,0:T(8,128)(2,1)} %x_in.1), custom_call_target="tpu_custom_call" | custom-call | tf_op jit(solution)/shard_map/pallas_call | solution.py:447
  110.4 3.6 %shard_map.42 = (f32[16,1,64,1024]{3,2,1,0:T(8,128)}, f32[16,1,64,1024]{3,2,1,0:T(8,128)}) custom-call(bf16[2,2,4,16,64,128]{5,4,3,2,1,0:T(8,128)(2,1)S(1)} %shard_map.41.stats), custom_call_target="tpu_custom_call" | custom-call | tf_op jit(solution)/shard_map/pallas_call | solution.py:470

commit v3 on v2

--- a/solution.py
+++ b/solution.py
@@ -1,5 +1,3 @@
-import heapq
-
 import jax
 import jax.numpy as jnp
 from jax import lax
@@ -16,32 +14,14 @@
 Q_AT = (0, 2, 3, 6, 7, 10, 11, 14)
 D_AT = (1, 4, 5, 8, 9, 12, 13, 15)
 OPP, OWN = 0, 1
-BLOCK = 0.0417
-
-
-def out_times(produced):
-    queue, free, landed, n = [], [0.0, 0.0], {}, 0
-    for tile, at in produced.items():
-        heapq.heappush(queue, (at, n, 0, tile))
-        n += 1
-    while queue:
-        at, _, hop, tile = heapq.heappop(queue)
-        link = tile[0] if hop == 0 else 1 - tile[0]
-        free[link] = max(free[link], at) + BLOCK * (tile[3] if tile[4] is None else tile[3] / 2)
-        if hop == 0:
-            landed[tile] = free[link] + 0.15
-            heapq.heappush(queue, (landed[tile], n, 1, tile))
-            n += 1
-    return landed
 
 
 N_RING = 16 + 12 + 4 + 16
-N_OUT = 58
-Z_SEND, X_SEND, Y_SEND, P_SEND, SHIP_SEND, RELAY_SEND = range(6)
+Z_SEND, X_SEND, Y_SEND, P_SEND, SHIP_SEND = range(5)
 
 
 def gather_kernel(
-    q_in, x_in, out, left, xs_left, right, ship, relay, send_sem, ring_sem, ship_sem, out_sem, local_sem
+    q_in, x_in, out, left, xs_left, right, ship, send_sem, ring_sem, out_sem, local_sem
 ):
     fd, tokens = q_in.shape
     half = fd // 2
@@ -60,7 +40,8 @@
     y_own = device(yh, z, 1 - yl, x, core)
 
     barrier = pltpu.get_barrier_semaphore()
-    neighbours = (z_up, z_down, x_up, x_down, partner, y_opp, y_own)
+    y_far = device(1 - yh, z, yl, x, core)
+    neighbours = (z_up, z_down, x_up, x_down, partner, y_opp, y_own, y_far)
     for d in neighbours:
         pl.semaphore_signal(barrier, inc=1, device_id=d, device_id_type=MESH)
     pl.semaphore_wait(barrier, len(neighbours))
@@ -145,21 +126,13 @@
         return [y_to_opp if hy == OPP else y_to_own] + got
 
     def block(ref, tile):
-        path, xs, r0, n, h = tile
+        ly, xs, r0, n, h = tile
         if h is None:
-            return ref.at[path, xs, pl.ds(r0, n)]
-        return ref.at[path, xs, pl.ds(r0, n), pl.ds(h * half, half)]
-
-    first, second = {}, {}
-
-    def plan(tile):
-        to = (y_opp, y_own)
-        first[tile] = copy(
-            block(ship, tile), block(relay, tile), SHIP_SEND, ship_sem.at[len(first)], to[tile[0]]
-        )
-        second[tile] = copy(
-            block(relay, tile), block(out.at[1], tile), RELAY_SEND, out_sem.at[0], to[1 - tile[0]]
-        )
+            return ref.at[ly, xs, pl.ds(r0, n)]
+        return ref.at[ly, xs, pl.ds(r0, n), pl.ds(h * half, half)]
+
+    def ship_out(tile):
+        copy(block(ship, tile), block(out.at[1], tile), SHIP_SEND, out_sem.at[0], y_far).start()
 
     have = set()
 
@@ -312,13 +285,11 @@
     at(4.25, far_arrived(((OPP, 1), (OPP, 0))))
     at(6.35, far_arrived(((OWN, 0), (OWN, 1))))
 
-    produced, pending, sent = {}, [], set()
+    pending = []
 
     def flush():
         while pending:
-            tile = pending.pop(0)
-            sent.add(tile)
-            first[tile].start()
+            ship_out(pending.pop(0))
 
     def opp_at(time, r0, n, xs, lys=(0, 1), h=None):
         tiles = [(ly, xs, r0, n, h) for ly in lys]
@@ -339,9 +310,6 @@
             pending.extend(tiles)
 
         at(time, go)
-        for tile in tiles:
-            plan(tile)
-            produced[tile] = time + 0.1
 
     def own_at(time, r0, n, start, step, count):
         def go():
@@ -380,24 +348,11 @@
     for h in (0, 1):
         for i, xs in enumerate((1, 0, 2, 3)):
             opp_at(6.60 + 0.5 * h + 0.05 * i, 14, 2, xs, (0, 1), h)
-    own_at(7.31, 14, 2, 0, 1, 3)
-    own_at(7.42, 0, 4, 3, 1, 1)
-    own_at(7.49, 4, 4, 3, 1, 1)
-    own_at(7.56, 8, 4, 3, 1, 1)
-    own_at(7.63, 12, 4, 3, 1, 1)
-    assert len(first) == N_OUT, len(first)
-
-    def relay_at(time, tile):
-        def go():
-            if tile not in sent:
-                flush()
-            need(first[tile])
-            second[tile].start()
-
-        at(time, go)
-
-    for tile, time in out_times(produced).items():
-        relay_at(time, tile)
+    own_at(6.52, 0, 4, 3, 1, 1)
+    own_at(6.55, 4, 4, 3, 1, 1)
+    own_at(6.85, 8, 4, 3, 1, 1)
+    own_at(6.90, 12, 2, 3, 1, 1)
+    own_at(7.31, 14, 2, 0, 1, 4)
 
     for _, _, fn in sorted(events, key=lambda e: e[:2]):
         fn()
@@ -405,13 +360,12 @@
     def finish(ref, sender):
         copy(ref, ref, sender, out_sem.at[0], z_up).wait_send()
 
-    copy(out.at[1], out.at[1], RELAY_SEND, out_sem.at[0], z_up).wait_recv()
+    copy(out.at[1], out.at[1], SHIP_SEND, out_sem.at[0], z_up).wait_recv()
     finish(left.at[pl.ds(0, 14)], Z_SEND)
     finish(left.at[pl.ds(0, 12)], X_SEND)
     finish(left.at[pl.ds(0, 3)], Y_SEND)
     finish(left.at[pl.ds(0, 16)], P_SEND)
     finish(ship, SHIP_SEND)
-    finish(relay, RELAY_SEND)
 
 
 def widen_kernel(stats, gram, cross, stage, sem):
@@ -454,10 +408,8 @@
             pltpu.VMEM((8, fd, tokens), BF16),
             pltpu.VMEM((4, 2, 2, 2, fd, tokens), BF16),
             pltpu.VMEM(half_out, BF16),
-            pltpu.VMEM(half_out, BF16),
-            pltpu.SemaphoreType.DMA((6,)),
+            pltpu.SemaphoreType.DMA((5,)),
             pltpu.SemaphoreType.DMA((N_RING,)),
-            pltpu.SemaphoreType.DMA((N_OUT,)),
             pltpu.SemaphoreType.DMA((1,)),
             pltpu.SemaphoreType.DMA((3,)),
         ],

time: 115 us -> 91.5 us (0.80)
  the two profiles are of different devices: /device:TPU:6 before, /device:TPU:1 now
where the time goes in v3:
time: 91.5 us; the launch traced here: 91.4 us
  Pallas kernels  90.6 us (99%)
    pallas_call x1, Pallas kernels, per_device(): pl.pallas_call(gather_kernel, out_shape=pltpu.VMEM((2,) + half_out, BF16)...  87 us
    pallas_call x1, Pallas kernels, per_device(): pl.pallas_call(widen_kernel, out_shape=[jax.ShapeDtypeStruct(shape, F32)]...  3.59 us

profile of v3, /device:TPU:1, one launch (start us, length us, event | category | flops | bytes accessed | tf_op | source)
XLA Modules:
  0.0 91.4 jit_solution(1162028677992189575)
XLA Ops:
  0.6 87.0 %shard_map.41.stats = bf16[2,2,4,16,64,128]{5,4,3,2,1,0:T(8,128)(2,1)S(1)} custom-call(bf16[64,3072]{1,0:T(8,128)(2,1)} %q_in.1, bf16[64,3072]{1,0:T(8,128)(2,1)} %x_in.1), custom_call_target="tpu_custom_call" | custom-call | tf_op jit(solution)/shard_map/pallas_call | solution.py:401
  87.7 3.6 %shard_map.42 = (f32[16,1,64,1024]{3,2,1,0:T(8,128)}, f32[16,1,64,1024]{3,2,1,0:T(8,128)}) custom-call(bf16[2,2,4,16,64,128]{5,4,3,2,1,0:T(8,128)(2,1)S(1)} %shard_map.41.stats), custom_call_target="tpu_custom_call" | custom-call | tf_op jit(solution)/shard_map/pallas_call | solution.py:422

commit v4 on v3

--- a/solution.py
+++ b/solution.py
@@ -16,7 +16,7 @@
 OPP, OWN = 0, 1
 
 
-N_RING = 16 + 12 + 4 + 16
+N_RING = 16 + 6 + 20 + 16
 Z_SEND, X_SEND, Y_SEND, P_SEND, SHIP_SEND = range(5)
 
 
@@ -91,21 +91,26 @@
             else:
                 z_msgs[up, 4, "x", h] = make(xs_left.at[6, rows], xs_left.at[7, rows], Z_SEND, to)
 
-    y_to_opp = make(q_in, right.at[1, OPP, 1, core], Y_SEND, y_opp)
-    y_to_own = make(q_in, right.at[1, OWN, 1, core], Y_SEND, y_own)
+    y_msgs = {}
+    for to, hy in ((y_opp, OPP), (y_own, OWN)):
+        for h in (lo, hi) if hy == OPP else (hi, lo):
+            y_msgs[hy, h is hi] = make(q_in.at[h], right.at[1, hy, 1, core, h], Y_SEND, to)
     y_two_a = make(right.at[1, OPP, 1, core, lo], right.at[1, OPP, 0, core, lo], Y_SEND, y_own)
     y_two_b = make(right.at[1, OWN, 1, core, hi], right.at[1, OPP, 0, core, hi], Y_SEND, y_opp)
 
     x_msgs = {}
     for hy in (OPP, OWN):
         for ly in (0, 1):
-            src = q_in if (hy, ly) == (OWN, 0) else right.at[1, hy, ly, core]
-            x_msgs["up", hy, ly] = make(src, right.at[0, hy, ly, core], X_SEND, x_up)
-            x_msgs["down", hy, ly] = make(src, right.at[2, hy, ly, core], X_SEND, x_down)
-    for hy, ly in ((OPP, 1), (OWN, 0)):
-        x_msgs["far", hy, ly] = make(right.at[0, hy, ly, core], right.at[3, hy, ly, core], X_SEND, x_up)
-    for hy, ly in ((OPP, 0), (OWN, 1)):
-        x_msgs["far", hy, ly] = make(right.at[2, hy, ly, core], right.at[3, hy, ly, core], X_SEND, x_down)
+            in_halves = (hy, ly) in ((OWN, 0), (OPP, 1))
+            for way, slot, to in (("up", 0, x_up), ("down", 2, x_down)):
+                x_msgs[way, hy, ly] = []
+                for h in (lo, hi) if in_halves else (pl.ds(0, fd),):
+                    src = q_in.at[h] if (hy, ly) == (OWN, 0) else right.at[1, hy, ly, core, h]
+                    x_msgs[way, hy, ly].append(make(src, right.at[slot, hy, ly, core, h], X_SEND, to))
+            x_msgs["far", hy, ly] = [
+                make(right.at[slot, hy, ly, core, h], right.at[3, hy, ly, core, h], X_SEND, to)
+                for slot, h, to in ((0, lo, x_up), (2, hi, x_down))
+            ]
 
     p_msgs = {}
     for xs in range(4):
@@ -120,10 +125,10 @@
     def right_messages(xs, hy, ly):
         got = [p_msgs[xs, hy, ly]]
         if xs != 1:
-            return [x_msgs[x_way[xs], hy, ly]] + got
+            return x_msgs[x_way[xs], hy, ly] + got
         if ly == 0:
             return ([y_two_a, y_two_b] if hy == OPP else []) + got
-        return [y_to_opp if hy == OPP else y_to_own] + got
+        return [y_msgs[hy, False], y_msgs[hy, True]] + got
 
     def block(ref, tile):
         ly, xs, r0, n, h = tile
@@ -221,10 +226,10 @@
     def start_all():
         for key in ((True, 1, "q"), (False, 1, "q")):
             z_msgs[key].start()
-        y_to_opp.start()
-        y_to_own.start()
-        x_msgs["up", OWN, 0].start()
-        x_msgs["down", OWN, 0].start()
+        for m in y_msgs.values():
+            m.start()
+        x_msgs["up", OWN, 0][0].start()
+        x_msgs["down", OWN, 0][0].start()
         p_msgs[1, OWN, 0].start()
         for key in ((True, 1, "x"), (False, 1, "x")):
             z_msgs[key].start()
@@ -233,57 +238,65 @@
 
     at(0.0, start_all)
 
-    def y_arrived():
-        need(y_to_opp)
+    def to_x(hy, ly, i=0):
+        x_msgs["up", hy, ly][i].start()
+        x_msgs["down", hy, ly][i].start()
+
+    def y_first_half():
+        need(y_msgs[OPP, False])
         y_two_a.start()
-        x_msgs["up", OPP, 1].start()
-        x_msgs["down", OPP, 1].start()
+        to_x(OPP, 1, 0)
+        need(y_msgs[OWN, True])
+        y_two_b.start()
+
+    at(0.55, y_first_half)
+
+    def y_second_half():
+        need(y_msgs[OPP, True])
+        to_x(OPP, 1, 1)
         p_msgs[1, OPP, 1].start()
-        need(y_to_own)
-        y_two_b.start()
+        need(y_msgs[OWN, False])
         p_msgs[1, OWN, 1].start()
 
-    at(1.04, y_arrived)
+    at(1.04, y_second_half)
 
     def y_two_arrived():
         need(y_two_a)
         need(y_two_b)
-        x_msgs["up", OPP, 0].start()
-        x_msgs["down", OPP, 0].start()
+        to_x(OPP, 0)
         p_msgs[1, OPP, 0].start()
 
     at(1.6, y_two_arrived)
 
-    def x_arrived(hy, ly, then=()):
+    def x_arrived(hy, ly):
         def go():
-            need(x_msgs["up", hy, ly])
-            if (hy, ly) == (OPP, 1):
-                x_msgs["far", hy, ly].start()
-            p_msgs[0, hy, ly].start()
-            need(x_msgs["down", hy, ly])
-            if (hy, ly) in ((OPP, 0), (OWN, 1)):
-                x_msgs["far", hy, ly].start()
-            p_msgs[2, hy, ly].start()
-            for m in then:
-                x_msgs[m].start()
+            for i, way in enumerate(("up", "down")):
+                for m in x_msgs[way, hy, ly]:
+                    need(m)
+                x_msgs["far", hy, ly][i].start()
+                p_msgs[2 * i, hy, ly].start()
 
         return go
 
-    at(1.06, x_arrived(OWN, 0))
-    at(2.15, x_arrived(OPP, 1, (("up", OWN, 1),)))
-    at(3.2, x_arrived(OPP, 0, (("down", OWN, 1), ("far", OWN, 0))))
-    at(5.3, x_arrived(OWN, 1))
-
-    def far_arrived(pairs):
+    at(1.65, x_arrived(OPP, 1))
+    at(2.70, x_arrived(OPP, 0))
+    at(2.71, lambda: to_x(OWN, 0, 1))
+    at(4.20, x_arrived(OWN, 0))
+    at(5.20, x_arrived(OWN, 1))
+
+    def far_arrived(hy, ly):
         def go():
-            for hy, ly in pairs:
-                need(x_msgs["far", hy, ly])
-                p_msgs[3, hy, ly].start()
+            for m in x_msgs["far", hy, ly]:
+                need(m)
+            p_msgs[3, hy, ly].start()
 
         return go
 
-    at(4.25, far_arrived(((OPP, 1), (OPP, 0))))
-    at(6.35, far_arrived(((OWN, 0), (OWN, 1))))
+    at(3.18, far_arrived(OPP, 1))
+    at(3.19, lambda: to_x(OWN, 1))
+    at(3.70, far_arrived(OPP, 0))
+    at(5.70, far_arrived(OWN, 0))
+    at(6.22, far_arrived(OWN, 1))
 
     pending = []
 
@@ -321,38 +334,38 @@
 
         at(time, go)
 
-    opp_at(1.75, 0, 2, 1)
-    own_at(1.76, 0, 2, 1, 1, 1)
-    opp_at(2.10, 2, 4, 1)
+    opp_at(1.25, 0, 4, 1, (1,))
+    own_at(1.35, 0, 4, 1, 1, 1)
+    opp_at(1.72, 0, 4, 1, (0,))
     for i, xs in enumerate((0, 2)):
-        opp_at(2.32 + 0.08 * i, 0, 6, xs, (1,))
-    own_at(2.50, 2, 4, 1, 1, 1)
-    opp_at(3.10, 6, 2, 1)
+        opp_at(1.80 + 0.08 * i, 0, 4, xs, (1,))
+    opp_at(2.10, 4, 2, 1)
     for i, xs in enumerate((0, 2)):
-        opp_at(3.36 + 0.13 * i, 0, 6, xs, (0,))
-        opp_at(3.44 + 0.13 * i, 6, 2, xs)
+        opp_at(2.18 + 0.08 * i, 4, 2, xs, (1,))
+    for i, xs in enumerate((0, 2)):
+        opp_at(2.82 + 0.10 * i, 0, 6, xs, (0,))
     for i, xs in enumerate((1, 0, 2)):
-        opp_at(4.10 + 0.05 * i, 8, 2, xs)
-    opp_at(4.42, 0, 4, 3)
-    opp_at(4.49, 4, 4, 3)
-    opp_at(4.56, 8, 2, 3)
-    own_at(4.70, 6, 4, 1, 1, 1)
+        opp_at(3.10 + 0.08 * i, 6, 2, xs)
+    opp_at(3.35, 0, 8, 3, (1,))
+    opp_at(3.85, 0, 8, 3, (0,))
+    own_at(3.95, 4, 4, 1, 1, 1)
     for i, xs in enumerate((1, 0, 2, 3)):
-        opp_at(5.10 + 0.05 * i, 10, 2, xs)
-    own_at(5.50, 0, 4, 0, 2, 2)
-    own_at(5.66, 4, 4, 0, 2, 2)
-    own_at(5.80, 8, 2, 0, 2, 2)
+        opp_at(4.10 + 0.08 * i, 8, 2, xs)
     for i, xs in enumerate((1, 0, 2, 3)):
-        opp_at(6.10 + 0.05 * i, 12, 2, xs)
-    own_at(6.31, 10, 4, 0, 1, 3)
-    for h in (0, 1):
-        for i, xs in enumerate((1, 0, 2, 3)):
-            opp_at(6.60 + 0.5 * h + 0.05 * i, 14, 2, xs, (0, 1), h)
-    own_at(6.52, 0, 4, 3, 1, 1)
-    own_at(6.55, 4, 4, 3, 1, 1)
-    own_at(6.85, 8, 4, 3, 1, 1)
-    own_at(6.90, 12, 2, 3, 1, 1)
-    own_at(7.31, 14, 2, 0, 1, 4)
+        opp_at(5.10 + 0.08 * i, 10, 2, xs)
+    own_at(5.45, 0, 4, 0, 2, 2)
+    own_at(5.60, 4, 4, 0, 2, 2)
+    own_at(5.76, 8, 4, 0, 1, 3)
+    for i, xs in enumerate((1, 0, 2, 3)):
+        opp_at(6.10 + 0.08 * i, 12, 2, xs)
+    own_at(6.43, 0, 4, 3, 1, 1)
+    own_at(6.51, 4, 4, 3, 1, 1)
+    for i, xs in enumerate((1, 0, 2, 3)):
+        opp_at(6.60 + 0.08 * i, 14, 2, xs, (0, 1), 0)
+    own_at(6.95, 8, 4, 3, 1, 1)
+    for i, xs in enumerate((1, 0, 2, 3)):
+        opp_at(7.10 + 0.08 * i, 14, 2, xs, (0, 1), 1)
+    own_at(7.45, 12, 4, 0, 1, 4)
 
     for _, _, fn in sorted(events, key=lambda e: e[:2]):
         fn()

time: 91.5 us -> 86.4 us (0.944)
  the two profiles are of different devices: /device:TPU:1 before, /device:TPU:6 now
where the time goes in v4:
time: 86.4 us; the launch traced here: 85.6 us
  Pallas kernels  84.8 us (98%)
    pallas_call x1, Pallas kernels, per_device(): pl.pallas_call(gather_kernel, out_shape=pltpu.VMEM((2,) + half_out, BF16)...  81.2 us
    pallas_call x1, Pallas kernels, per_device(): pl.pallas_call(widen_kernel, out_shape=[jax.ShapeDtypeStruct(shape, F32)]...  3.59 us

profile of v4, /device:TPU:6, one launch (start us, length us, event | category | flops | bytes accessed | tf_op | source)
XLA Modules:
  0.0 85.6 jit_solution(7307777910373664640)
XLA Ops:
  0.6 81.2 %shard_map.41.stats = bf16[2,2,4,16,64,128]{5,4,3,2,1,0:T(8,128)(2,1)S(1)} custom-call(bf16[64,3072]{1,0:T(8,128)(2,1)} %q_in.1, bf16[64,3072]{1,0:T(8,128)(2,1)} %x_in.1), custom_call_target="tpu_custom_call" | custom-call | tf_op jit(solution)/shard_map/pallas_call | solution.py:414
  81.8 3.6 %shard_map.42 = (f32[16,1,64,1024]{3,2,1,0:T(8,128)}, f32[16,1,64,1024]{3,2,1,0:T(8,128)}) custom-call(bf16[2,2,4,16,64,128]{5,4,3,2,1,0:T(8,128)(2,1)S(1)} %shard_map.41.stats), custom_call_target="tpu_custom_call" | custom-call | tf_op jit(solution)/shard_map/pallas_call | solution.py:435

commit v5 on v4

--- a/solution.py
+++ b/solution.py
@@ -16,12 +16,12 @@
 OPP, OWN = 0, 1
 
 
-N_RING = 16 + 6 + 20 + 16
+N_RING = 18 + 6 + 20 + 16
 Z_SEND, X_SEND, Y_SEND, P_SEND, SHIP_SEND = range(5)
 
 
 def gather_kernel(
-    q_in, x_in, out, left, xs_left, right, ship, send_sem, ring_sem, out_sem, local_sem
+    q_in, x_in, out, left, xs_left, right, ship, opp_part, own_part, send_sem, ring_sem, out_sem, local_sem
 ):
     fd, tokens = q_in.shape
     half = fd // 2
@@ -71,10 +71,12 @@
     locals_ = [
         pltpu.make_async_copy(q_in, left.at[0], local_sem.at[0]),
         pltpu.make_async_copy(x_in, xs_left.at[0], local_sem.at[1]),
-        pltpu.make_async_copy(q_in, right.at[1, OWN, 0, core], local_sem.at[2]),
+        pltpu.make_async_copy(q_in, right.at[OWN, 1, 0, core], local_sem.at[2]),
     ]
 
-    lo, hi = pl.ds(0, half), pl.ds(half, half)
+    lo, hi, rows_all = pl.ds(0, half), pl.ds(half, half), pl.ds(0, fd)
+    early, late, all_tokens = pl.ds(0, tokens // 2), pl.ds(tokens // 2, tokens // 2), pl.ds(0, tokens)
+    pieces = ((lo, all_tokens), (hi, early), (hi, late))
 
     z_msgs = {}
     for up in (True, False):
@@ -85,18 +87,18 @@
             x_src = x_in if k == 1 else xs_left.at[src]
             z_msgs[up, k, "q"] = make(q_src, left.at[Q_AT[dst]], Z_SEND, to)
             z_msgs[up, k, "x"] = make(x_src, xs_left.at[dst], Z_SEND, to)
-        for h, rows in enumerate((lo, hi)):
+        for i, cut in enumerate(pieces):
             if up:
-                z_msgs[up, 4, "q", h] = make(left.at[Q_AT[5], rows], left.at[Q_AT[7], rows], Z_SEND, to)
+                z_msgs[up, 4, "q", i] = make(left.at[Q_AT[5], *cut], left.at[Q_AT[7], *cut], Z_SEND, to)
             else:
-                z_msgs[up, 4, "x", h] = make(xs_left.at[6, rows], xs_left.at[7, rows], Z_SEND, to)
+                z_msgs[up, 4, "x", i] = make(xs_left.at[6, *cut], xs_left.at[7, *cut], Z_SEND, to)
 
     y_msgs = {}
     for to, hy in ((y_opp, OPP), (y_own, OWN)):
         for h in (lo, hi) if hy == OPP else (hi, lo):
-            y_msgs[hy, h is hi] = make(q_in.at[h], right.at[1, hy, 1, core, h], Y_SEND, to)
-    y_two_a = make(right.at[1, OPP, 1, core, lo], right.at[1, OPP, 0, core, lo], Y_SEND, y_own)
-    y_two_b = make(right.at[1, OWN, 1, core, hi], right.at[1, OPP, 0, core, hi], Y_SEND, y_opp)
+            y_msgs[hy, h is hi] = make(q_in.at[h], right.at[hy, 1, 1, core, h], Y_SEND, to)
+    y_two_a = make(right.at[OPP, 1, 1, core, lo], right.at[OPP, 1, 0, core, lo], Y_SEND, y_own)
+    y_two_b = make(right.at[OWN, 1, 1, core, hi], right.at[OPP, 1, 0, core, hi], Y_SEND, y_opp)
 
     x_msgs = {}
     for hy in (OPP, OWN):
@@ -105,10 +107,10 @@
             for way, slot, to in (("up", 0, x_up), ("down", 2, x_down)):
                 x_msgs[way, hy, ly] = []
                 for h in (lo, hi) if in_halves else (pl.ds(0, fd),):
-                    src = q_in.at[h] if (hy, ly) == (OWN, 0) else right.at[1, hy, ly, core, h]
-                    x_msgs[way, hy, ly].append(make(src, right.at[slot, hy, ly, core, h], X_SEND, to))
+                    src = q_in.at[h] if (hy, ly) == (OWN, 0) else right.at[hy, 1, ly, core, h]
+                    x_msgs[way, hy, ly].append(make(src, right.at[hy, slot, ly, core, h], X_SEND, to))
             x_msgs["far", hy, ly] = [
-                make(right.at[slot, hy, ly, core, h], right.at[3, hy, ly, core, h], X_SEND, to)
+                make(right.at[hy, slot, ly, core, h], right.at[hy, 3, ly, core, h], X_SEND, to)
                 for slot, h, to in ((0, lo, x_up), (2, hi, x_down))
             ]
 
@@ -116,8 +118,8 @@
     for xs in range(4):
         for hy in (OPP, OWN):
             for ly in (0, 1):
-                src = q_in if (xs, hy, ly) == (1, OWN, 0) else right.at[xs, hy, ly, core]
-                p_msgs[xs, hy, ly] = make(src, right.at[xs, hy, ly, core], P_SEND, partner)
+                src = q_in if (xs, hy, ly) == (1, OWN, 0) else right.at[hy, xs, ly, core]
+                p_msgs[xs, hy, ly] = make(src, right.at[hy, xs, ly, core], P_SEND, partner)
     assert ring_count[0] == N_RING, ring_count[0]
 
     x_way = {0: "up", 2: "down", 3: "far"}
@@ -146,18 +148,18 @@
             have.add(key)
             fn()
 
-    def subtract(slot, rows):
-        left[D_AT[slot], rows] = (xs_left[slot, rows].astype(F32) - left[Q_AT[slot], rows].astype(F32)).astype(
-            BF16
-        )
-
-    def left_ready(r0, n, h):
+    def subtract(slot, rows, cols):
+        left[D_AT[slot], rows, cols] = (
+            xs_left[slot, rows, cols].astype(F32) - left[Q_AT[slot], rows, cols].astype(F32)
+        ).astype(BF16)
+
+    def left_ready(r0, n, parts=(0, 1, 2)):
         for r in range(r0, r0 + n):
             if r >= 14:
-                for i in (0, 1) if h is None else (h,):
+                for i in parts:
                     need(z_msgs[True, 4, "q", i])
                     need(z_msgs[False, 4, "x", i])
-                    once(("d", 7, i), lambda i=i: subtract(7, pl.ds(i * half, half)))
+                    once(("d", 7, i), lambda i=i: subtract(7, *pieces[i]))
             elif r == 0:
                 once("q", locals_[0].wait)
             elif r in Q_AT:
@@ -171,7 +173,7 @@
                 else:
                     need(z_msgs[slot % 2 == 1, (slot + 1) // 2, "q"])
                     need(z_msgs[slot % 2 == 1, (slot + 1) // 2, "x"])
-                once(("d", slot), lambda slot=slot: subtract(slot, pl.ds(0, fd)))
+                once(("d", slot), lambda slot=slot: subtract(slot, rows_all, all_tokens))
 
     def right_ready(xs, hy, lys):
         for ly in lys:
@@ -180,27 +182,32 @@
             for m in right_messages(xs, hy, ly):
                 need(m)
 
-    def product(xs, hy, lys, r0, n, h):
-        if h is None:
-            a = left[r0 : r0 + n].reshape(n * fd, tokens)
-        else:
-            a = left[r0 : r0 + n, h * half : (h + 1) * half].reshape(n * half, tokens)
-        b = right[xs, hy, lys[0] : lys[-1] + 1].reshape(len(lys) * 2 * fd, tokens)
-        p = lax.dot_general(a, b, (((1,), (1,)), ((), ())), preferred_element_type=F32) * scale
-        return p.astype(BF16).reshape(n, fd if h is None else half, len(lys) * 2 * fd)
-
-    def own_tiles(r0, n, start, step, count):
-        def one(i, _):
-            xs = start + i * step
-            p = product(xs, OWN, (0, 1), r0, n, None)
+    def dot(hy, xs, nx, lys, r0, n, h=None, cols=None):
+        rows = slice(0, fd) if h is None else slice(h * half, (h + 1) * half)
+        cols = slice(0, tokens) if cols is None else cols
+        a = left[r0 : r0 + n, rows, cols]
+        a = a.reshape(-1, a.shape[-1])
+        b = right[hy, xs : xs + nx, lys[0] : lys[-1] + 1, :, :, cols]
+        b = b.reshape(-1, b.shape[-1])
+        return lax.dot_general(a, b, (((1,), (1,)), ((), ())), preferred_element_type=F32)
+
+    def rounded(p, n):
+        return (p * scale).astype(BF16).reshape(n, p.shape[0] // n, p.shape[1])
+
+    def put_own(p, r0, n, xs, nx):
+        p = rounded(p, n)
+        for i in range(nx):
             for ly in (0, 1):
-                out[0, ly, xs, r0 : r0 + n] = p[..., ly * 2 * fd : (ly + 1) * 2 * fd]
-            return 0
-
-        if count == 1:
-            one(0, 0)
-        else:
-            lax.fori_loop(0, count, one, 0)
+                at = (2 * i + ly) * 2 * fd
+                out[0, ly, xs + i, r0 : r0 + n] = p[..., at : at + 2 * fd]
+
+    def put_ship(p, r0, n, xs, nx, lys, h):
+        p = rounded(p, n)
+        rows = slice(0, fd) if h is None else slice(h * half, (h + 1) * half)
+        for i in range(nx):
+            for j, ly in enumerate(lys):
+                at = (len(lys) * i + j) * 2 * fd
+                ship[ly, xs + i, r0 : r0 + n, rows] = p[..., at : at + 2 * fd]
 
     events = []
 
@@ -214,8 +221,8 @@
                 if k < 3:
                     z_msgs[up, k + 1, what].start()
                 elif up == (what == "q"):
-                    z_msgs[up, 4, what, 0].start()
-                    z_msgs[up, 4, what, 1].start()
+                    for i in range(3):
+                        z_msgs[up, 4, what, i].start()
 
         return go
 
@@ -304,68 +311,84 @@
         while pending:
             ship_out(pending.pop(0))
 
-    def opp_at(time, r0, n, xs, lys=(0, 1), h=None):
-        tiles = [(ly, xs, r0, n, h) for ly in lys]
-
+    def opp_at(time, r0, n, xs, nx=1, lys=(0, 1), h=None):
         def go():
-            left_ready(r0, n, h)
-            right_ready(xs, OPP, lys)
+            left_ready(r0, n, (0, 1, 2) if h is None else (h,))
+            for i in range(nx):
+                right_ready(xs + i, OPP, lys)
             before = list(pending)
-            p = product(xs, OPP, lys, r0, n, h)
-            for i, tile in enumerate(tiles):
-                value = p[..., i * 2 * fd : (i + 1) * 2 * fd]
-                if h is None:
-                    ship[tile[0], xs, r0 : r0 + n] = value
-                else:
-                    ship[tile[0], xs, r0 : r0 + n, h * half : (h + 1) * half] = value
+            put_ship(dot(OPP, xs, nx, lys, r0, n, h), r0, n, xs, nx, lys, h)
             if before:
                 flush()
-            pending.extend(tiles)
+            pending.extend((ly, xs + i, r0, n, h) for i in range(nx) for ly in lys)
 
         at(time, go)
 
-    def own_at(time, r0, n, start, step, count):
+    def own_at(time, r0, n, xs, nx=1):
         def go():
-            left_ready(r0, n, None)
-            for i in range(count):
-                right_ready(start + i * step, OWN, (0, 1))
-            own_tiles(r0, n, start, step, count)
+            left_ready(r0, n)
+            for i in range(nx):
+                right_ready(xs + i, OWN, (0, 1))
+            put_own(dot(OWN, xs, nx, (0, 1), r0, n), r0, n, xs, nx)
             flush()
 
         at(time, go)
 
-    opp_at(1.25, 0, 4, 1, (1,))
-    own_at(1.35, 0, 4, 1, 1, 1)
-    opp_at(1.72, 0, 4, 1, (0,))
+    def last_early():
+        left_ready(14, 2, (0, 1))
+        cols = slice(0, tokens // 2)
+        for xs in (0, 2):
+            span = slice(xs * 4 * fd, (xs + 2) * 4 * fd)
+            opp_part[:, span] = dot(OPP, xs, 2, (0, 1), 14, 2, 1, cols)
+        flush()
+        for xs in (0, 2):
+            for i in (0, 1):
+                right_ready(xs + i, OWN, (0, 1))
+            span = slice(xs * 4 * fd, (xs + 2) * 4 * fd)
+            own_part[:, span] = dot(OWN, xs, 2, (0, 1), 12, 4, None, cols)
+
+    def last_late():
+        left_ready(14, 2)
+        cols = slice(tokens // 2, tokens)
+        for xs in (0, 2):
+            span = slice(xs * 4 * fd, (xs + 2) * 4 * fd)
+            p = opp_part[:, span] + dot(OPP, xs, 2, (0, 1), 14, 2, 1, cols)
+            put_ship(p, 14, 2, xs, 2, (0, 1), 1)
+            flush()
+            pending.extend((ly, xs + i, 14, 2, 1) for i in (0, 1) for ly in (0, 1))
+        for xs in (0, 2):
+            span = slice(xs * 4 * fd, (xs + 2) * 4 * fd)
+            p = own_part[:, span] + dot(OWN, xs, 2, (0, 1), 12, 4, None, cols)
+            put_own(p, 12, 4, xs, 2)
+            flush()
+
+    opp_at(1.25, 0, 4, 1, 1, (1,))
+    own_at(1.35, 0, 4, 1)
+    opp_at(1.72, 0, 4, 1, 1, (0,))
     for i, xs in enumerate((0, 2)):
-        opp_at(1.80 + 0.08 * i, 0, 4, xs, (1,))
+        opp_at(1.80 + 0.08 * i, 0, 4, xs, 1, (1,))
     opp_at(2.10, 4, 2, 1)
     for i, xs in enumerate((0, 2)):
-        opp_at(2.18 + 0.08 * i, 4, 2, xs, (1,))
+        opp_at(2.18 + 0.08 * i, 4, 2, xs, 1, (1,))
     for i, xs in enumerate((0, 2)):
-        opp_at(2.82 + 0.10 * i, 0, 6, xs, (0,))
-    for i, xs in enumerate((1, 0, 2)):
-        opp_at(3.10 + 0.08 * i, 6, 2, xs)
-    opp_at(3.35, 0, 8, 3, (1,))
-    opp_at(3.85, 0, 8, 3, (0,))
-    own_at(3.95, 4, 4, 1, 1, 1)
-    for i, xs in enumerate((1, 0, 2, 3)):
-        opp_at(4.10 + 0.08 * i, 8, 2, xs)
-    for i, xs in enumerate((1, 0, 2, 3)):
-        opp_at(5.10 + 0.08 * i, 10, 2, xs)
-    own_at(5.45, 0, 4, 0, 2, 2)
-    own_at(5.60, 4, 4, 0, 2, 2)
-    own_at(5.76, 8, 4, 0, 1, 3)
-    for i, xs in enumerate((1, 0, 2, 3)):
-        opp_at(6.10 + 0.08 * i, 12, 2, xs)
-    own_at(6.43, 0, 4, 3, 1, 1)
-    own_at(6.51, 4, 4, 3, 1, 1)
-    for i, xs in enumerate((1, 0, 2, 3)):
-        opp_at(6.60 + 0.08 * i, 14, 2, xs, (0, 1), 0)
-    own_at(6.95, 8, 4, 3, 1, 1)
-    for i, xs in enumerate((1, 0, 2, 3)):
-        opp_at(7.10 + 0.08 * i, 14, 2, xs, (0, 1), 1)
-    own_at(7.45, 12, 4, 0, 1, 4)
+        opp_at(2.82 + 0.10 * i, 0, 6, xs, 1, (0,))
+    opp_at(3.10, 6, 2, 0, 2)
+    opp_at(3.17, 6, 2, 2)
+    opp_at(3.35, 0, 8, 3, 1, (1,))
+    opp_at(3.85, 0, 8, 3, 1, (0,))
+    own_at(3.95, 4, 4, 1)
+    for i, xs in enumerate((0, 2)):
+        opp_at(4.10 + 0.15 * i, 8, 2, xs, 2)
+        opp_at(5.10 + 0.15 * i, 10, 2, xs, 2)
+        opp_at(6.10 + 0.15 * i, 12, 2, xs, 2)
+        opp_at(6.60 + 0.12 * i, 14, 2, xs, 2, (0, 1), 0)
+    own_at(5.42, 0, 8, 0)
+    own_at(5.55, 0, 8, 2)
+    own_at(5.76, 8, 4, 0, 2)
+    own_at(6.43, 0, 8, 3)
+    at(6.85, last_early)
+    at(7.05, last_late)
+    own_at(7.30, 8, 4, 2, 2)
 
     for _, _, fn in sorted(events, key=lambda e: e[:2]):
         fn()
@@ -419,8 +442,10 @@
         scratch_shapes=[
             pltpu.VMEM((16, fd, tokens), BF16),
             pltpu.VMEM((8, fd, tokens), BF16),
-            pltpu.VMEM((4, 2, 2, 2, fd, tokens), BF16),
+            pltpu.VMEM((2, 4, 2, 2, fd, tokens), BF16),
             pltpu.VMEM(half_out, BF16),
+            pltpu.VMEM((fd, columns), F32),
+            pltpu.VMEM((4 * fd, columns), F32),
             pltpu.SemaphoreType.DMA((5,)),
             pltpu.SemaphoreType.DMA((N_RING,)),
             pltpu.SemaphoreType.DMA((1,)),

time: 86.4 us -> 84.5 us (0.978); the launches traced: 85.6 us -> 82.8 us
  Pallas kernels: 84.8 us -> 82 us
    pallas_call x1, Pallas kernels: 81.2 us -> 78.4 us  [per_device(): pl.pallas_call(gather_kernel, out_shape=pltpu.VMEM((2,) + half_out, BF16)...]
where the time goes in v5:
time: 84.5 us; the launch traced here: 82.8 us
  Pallas kernels  82 us (97%)
    pallas_call x1, Pallas kernels, per_device(): pl.pallas_call(gather_kernel, out_shape=pltpu.VMEM((2,) + half_out, BF16)...  78.4 us
    pallas_call x1, Pallas kernels, per_device(): pl.pallas_call(widen_kernel, out_shape=[jax.ShapeDtypeStruct(shape, F32)]...  3.59 us

profile of v5, /device:TPU:6, one launch (start us, length us, event | category | flops | bytes accessed | tf_op | source)
XLA Modules:
  0.0 82.8 jit_solution(1030206023325583617)
XLA Ops:
  0.6 78.4 %shard_map.41.stats = bf16[2,2,4,16,64,128]{5,4,3,2,1,0:T(8,128)(2,1)S(1)} custom-call(bf16[64,3072]{1,0:T(8,128)(2,1)} %q_in.1, bf16[64,3072]{1,0:T(8,128)(2,1)} %x_in.1), custom_call_target="tpu_custom_call" | custom-call | tf_op jit(solution)/shard_map/pallas_call | solution.py:437
  79.0 3.6 %shard_map.42 = (f32[16,1,64,1024]{3,2,1,0:T(8,128)}, f32[16,1,64,1024]{3,2,1,0:T(8,128)}) custom-call(bf16[2,2,4,16,64,128]{5,4,3,2,1,0:T(8,128)(2,1)S(1)} %shard_map.41.stats), custom_call_target="tpu_custom_call" | custom-call | tf_op jit(solution)/shard_map/pallas_call | solution.py:460
